TPU v7x, 256 devices: a whole 4x4x8 slice. The times are simulated.
256 devices in a mesh: depth: 32 (over z, x_hi, core), shot: 8 (over y, x_lo).
Axes of the slice: x: 4 (x_hi: 2, x_lo: 2; x = x_hi * 2 + x_lo), y: 4, z: 8, core: 2. Of those that a mesh axis runs over, the one named last changes fastest.
Arguments:
- courant: float32 [512, 64, 128], P('depth'), may hold values from 0.04 to 0.2
- wave_before: float32 [8, 512, 64, 128], P('shot', 'depth'), may hold values from -10 to 10
- wave_current: float32 [8, 512, 64, 128], P('shot', 'depth'), may hold values from -10 to 10
- adjoint_after: float32 [8, 512, 64, 128], P('shot', 'depth'), may hold values from -10 to 10
- adjoint_current: float32 [8, 512, 64, 128], P('shot', 'depth'), may hold values from -10 to 10
- source_cell: int32 [8], P('shot'), may hold values from 0 to 4194303
- wavelet: float32 [8, 4], P('shot'), may hold values from -15 to 15
- receiver_cell: int32 [8, 256], P('shot'), may hold values from 0 to 4194303
- residual: float32 [8, 4, 256], P('shot'), may hold values from -12 to 12
- history: float32 [2, 5, 512, 64, 128], P(None, None, 'depth', 'shot'), may hold values from -23 to 23, as said below
Outputs:
- gradient: float32 [512, 64, 128], P('depth', 'shot')
- direction: float32 [512, 64, 128], P('depth', 'shot')
- courant_next: float32 [512, 64, 128], P('depth')
Inputs may be any that keep to these rules, and one draw needn't show every extreme that they name: In every pair the sum over all cells of history[0] times history[1] is positive.
All inputs are finite; a program needn't handle non-finite values.
Results may differ from a plain program's by a relative error of at most 0.00026.
Values sent between devices are 32-bit elements; how exact they have to be, the bound alone decides.
A program may use at most 128 MiB of HBM per device.

v0:
```python
import jax
import jax.numpy as jnp
from jax import lax
from jax.sharding import PartitionSpec as P

STEPS = 4
PAIRS = 5
coefficients = (-205.0 / 72.0, 8.0 / 5.0, -1.0 / 5.0, 8.0 / 315.0, -1.0 / 560.0)


def with_halo(cells, sides, width):
    for axis, dim in sides:
        count = lax.axis_size(axis)
        ends = count - 1
        head = lax.slice_in_dim(cells, 0, width, axis=dim)
        tail = lax.slice_in_dim(cells, cells.shape[dim] - width, cells.shape[dim], axis=dim)
        cells = jnp.concatenate(
            [
                lax.ppermute(tail, axis, [(i, (i + 1) % count) for i in range(ends)]),
                cells,
                lax.ppermute(head, axis, [((i + 1) % count, i) for i in range(ends)]),
            ],
            axis=dim,
        )
    return cells


def laplace_core(extended):
    interior = extended[4:-4]
    count_rows = interior.shape[0]
    width_x = interior.shape[1]
    width_y = interior.shape[2]
    padded = jnp.pad(interior, ((0, 0), (4, 4), (4, 4)))
    summed = 3.0 * coefficients[0] * interior
    for reach in range(1, 5):
        weight = coefficients[reach]
        summed = summed + weight * (
            extended[4 + reach : 4 + reach + count_rows]
            + extended[4 - reach : 4 - reach + count_rows]
        )
        summed = summed + weight * (
            padded[:, 4 + reach : 4 + reach + width_x, 4 : 4 + width_y]
            + padded[:, 4 - reach : 4 - reach + width_x, 4 : 4 + width_y]
        )
        summed = summed + weight * (
            padded[:, 4 : 4 + width_x, 4 + reach : 4 + reach + width_y]
            + padded[:, 4 : 4 + width_x, 4 - reach : 4 - reach + width_y]
        )
    return summed


def inject(volume, cell_ids, values, offset):
    count_rows = volume.shape[0]
    plane_size = volume.shape[1] * volume.shape[2]
    depth_row = cell_ids // plane_size - offset
    remainder = cell_ids % plane_size
    inside = (depth_row >= 0) & (depth_row < count_rows)
    row_safe = jnp.clip(depth_row, 0, count_rows - 1)
    return volume.at[row_safe, remainder // volume.shape[2], remainder % volume.shape[2]].add(
        jnp.where(inside, values, jnp.zeros_like(values))
    )


def per_device(
    courant,
    wave_before,
    wave_current,
    adjoint_after,
    adjoint_current,
    source_cell,
    wavelet,
    receiver_cell,
    residual,
    history,
):
    slab_rows = courant.shape[0]
    first_row = lax.axis_index("depth") * slab_rows
    shot_count = lax.axis_size("shot")
    summed = jnp.zeros(courant.shape, jnp.float32)
    laplacians = []
    wave_old = wave_before[0]
    wave_now = wave_current[0]
    for moment in range(STEPS):
        extended = with_halo(wave_now, (("depth", 0),), 4)
        laplacian = laplace_core(extended)
        wave_new = 2.0 * wave_now - wave_old + courant * laplacian
        wave_new = inject(wave_new, source_cell, wavelet[0, moment : moment + 1], first_row)
        laplacians.append(laplacian)
        wave_old, wave_now = (wave_now, wave_new)
    adjoint_old = adjoint_after[0]
    adjoint_now = adjoint_current[0]
    for moment in reversed(range(STEPS)):
        extended = with_halo(courant * adjoint_now, (("depth", 0),), 4)
        adjoint_new = 2.0 * adjoint_now - adjoint_old + laplace_core(extended)
        adjoint_new = inject(adjoint_new, receiver_cell[0], residual[0, moment], first_row)
        summed = summed + adjoint_new * laplacians[moment]
        adjoint_old, adjoint_now = (adjoint_now, adjoint_new)
    grad_piece = lax.psum_scatter(summed, "shot", scatter_dimension=1, tiled=True) * (
        1.0 / (shot_count * STEPS)
    )
    displaced = history[0]
    changes = history[1]
    step_change = jnp.einsum("izxy,jzxy->ij", displaced, changes, precision=lax.Precision.HIGHEST)
    change_change = jnp.einsum("izxy,jzxy->ij", changes, changes, precision=lax.Precision.HIGHEST)
    step_grad = jnp.sum(displaced * grad_piece, axis=(1, 2, 3))
    change_grad = jnp.sum(changes * grad_piece, axis=(1, 2, 3))
    packed = jnp.concatenate(
        [step_change, change_change, step_grad[None], change_grad[None]], axis=0
    )
    packed = lax.psum(packed, ("depth", "shot"))
    step_change = packed[:PAIRS]
    change_change = packed[PAIRS : 2 * PAIRS]
    step_grad = packed[2 * PAIRS]
    change_grad = packed[2 * PAIRS + 1]
    inverse = [1.0 / step_change[i, i] for i in range(PAIRS)]
    alphas = [None] * PAIRS
    for i in reversed(range(PAIRS)):
        value = step_grad[i]
        for j in range(i + 1, PAIRS):
            value = value - alphas[j] * step_change[i, j]
        alphas[i] = inverse[i] * value
    gamma = step_change[PAIRS - 1, PAIRS - 1] / change_change[PAIRS - 1, PAIRS - 1]
    gains = []
    for i in range(PAIRS):
        value = change_grad[i]
        for j in range(PAIRS):
            value = value - alphas[j] * change_change[i, j]
        value = gamma * value
        for j in range(i):
            value = value + gains[j] * step_change[j, i]
        gains.append(alphas[i] - inverse[i] * value)
    scaled = grad_piece
    for i in range(PAIRS):
        scaled = scaled - alphas[i] * changes[i]
    scaled = gamma * scaled
    for i in range(PAIRS):
        scaled = scaled + gains[i] * displaced[i]
    direction = -scaled
    piece_width = grad_piece.shape[1]
    own_courant = lax.dynamic_slice_in_dim(
        courant, lax.axis_index("shot") * piece_width, piece_width, 1
    )
    next_piece = own_courant + 0.05 * direction
    courant_next = lax.all_gather(next_piece, "shot", axis=1, tiled=True)
    return (grad_piece, direction, courant_next)


def solution(mesh):
    return jax.shard_map(
        per_device,
        mesh=mesh,
        in_specs=(
            P("depth", None, None),
            P("shot", "depth", None, None),
            P("shot", "depth", None, None),
            P("shot", "depth", None, None),
            P("shot", "depth", None, None),
            P("shot"),
            P("shot", None),
            P("shot", None),
            P("shot", None, None),
            P(None, None, "depth", "shot", None),
        ),
        out_specs=(P("depth", "shot", None), P("depth", "shot", None), P("depth", None, None)),
        check_vma=False,
    )
```

profile of v0, /device:TPU:32, one launch (start us, length us, event | category | flops | bytes accessed | tf_op | source)
XLA Modules:
  0.0 397.9 jit_solution(11437620847095359479)
XLA Ops:
  7.2 1.3 bitcast_multiply_fusion
  8.6 4.0 %collective-permute-start = (f32[4,64,128]{2,1,0:T(8,128)S(1)}, f32[4,64,128]{2,1,0:T(8,128)S(1)}, u32[]{:S(2)}, u32[]{:S(2)}) collective-permute-start(f32[4,64,128]{2,1,0:T(8,128)S(1)} %get-tuple-element.70), channel_id=1, source_target_pairs={{8,0},{16,8},{24,16},{32,24},{40,32},{48,40},{56,48},{64,56},{72,6... | collective-permute-start | bytes 393224 | tf_op jit(solution)/shard_map/ppermute | solution.py:21
  12.7 1.9 collective-permute-start.1
  14.7 6.0 %collective-permute-start.2 = (f32[4,64,128]{2,1,0:T(8,128)S(1)}, f32[4,64,128]{2,1,0:T(8,128)S(1)}, u32[]{:S(2)}, u32[]{:S(2)}) collective-permute-start(f32[4,64,128]{2,1,0:T(8,128)S(1)} %get-tuple-element.68), channel_id=1, source_target_pairs={{8,0},{16,8},{24,16},{32,24},{40,32},{48,40},{56,48},{64,56},{72,6... | collective-permute-start | bytes 393224 | tf_op jit(solution)/shard_map/ppermute | solution.py:21
  20.7 1.9 collective-permute-start.3
  23.3 0.7 fusion.369
  26.7 0.7 and_reduce_fusion
  27.4 1.9 fusion.184
  29.4 23.9 %scatter_fusion = f32[16,64,128]{2,1,0:T(8,128)S(1)} fusion(f32[16,64,128]{2,1,0:T(8,128)S(1)} %fusion.184, s32[256]{0:T(256)S(1)} %bitcast.180, f32[256]{0:T(256)} %get-tuple-element.128), kind=kCustom, calls=%fused_computation | custom fusion | flops 256 | bytes 6144 | tf_op jit(solution)/shard_map/scatter-add | solution.py:59
  53.4 3.7 fusion.348
  57.0 0.7 dynamic-slice.24
  59.8 6.1 %collective-permute-start.10 = (f32[4,64,128]{2,1,0:T(8,128)S(1)}, f32[4,64,128]{2,1,0:T(8,128)S(1)}, u32[]{:S(2)}, u32[]{:S(2)}) collective-permute-start(f32[4,64,128]{2,1,0:T(8,128)S(1)} %get-tuple-element.59), channel_id=1, source_target_pairs={{8,0},{16,8},{24,16},{32,24},{40,32},{48,40},{56,48},{64,56},{72,6... | collective-permute-start | bytes 393224 | tf_op jit(solution)/shard_map/ppermute | solution.py:21
  65.9 1.9 collective-permute-start.11
  67.8 0.7 fusion.363
  68.5 6.0 %collective-permute-start.4 = (f32[4,64,128]{2,1,0:T(8,128)}, f32[4,64,128]{2,1,0:T(8,128)S(1)}, u32[]{:S(2)}, u32[]{:S(2)}) collective-permute-start(f32[4,64,128]{2,1,0:T(8,128)} %get-tuple-element.66), channel_id=1, source_target_pairs={{8,0},{16,8},{24,16},{32,24},{40,32},{48,40},{56,48},{64,56},{72,6... | collective-permute-start | bytes 393224 | tf_op jit(solution)/shard_map/ppermute | solution.py:21
  74.5 1.9 collective-permute-start.5
  76.5 9.1 %fusion.59 = f32[16,64,128]{2,1,0:T(8,128)S(1)} fusion(f32[16,64,128]{2,1,0:T(8,128)} %copy-done.6, f32[4,64,128]{2,1,0:T(8,128)S(1)} %collective-permute-done.11, f32[4,64,128]{2,1,0:T(8,128)S(1)} %collective-permute-done.10, f32[1,16,64,128]{3,2,1,0:T(8,128)S(1)} %copy-done.2, f32[16,64,128]{2,1,0:T(8,128)S(1)} %scatter_fusion), kind=kLoop, calls=%fused_computation.289 | loop fusion | flops 6291456 | bytes 2359296 | tf_op jit(solution)/shard_map/add | solution.py:94
  85.6 15.2 %scatter_fusion.1 = f32[16,64,128]{2,1,0:T(8,128)S(1)} fusion(f32[16,64,128]{2,1,0:T(8,128)S(1)} %fusion.59, s32[256]{0:T(256)S(1)} %bitcast.181, f32[256]{0:T(256)S(1)} %get-tuple-element.127), kind=kCustom, calls=%fused_computation.1 | custom fusion | flops 256 | bytes 6144 | tf_op jit(solution)/shard_map/scatter-add | solution.py:59
  100.9 2.7 multiply_add_fusion.1
  103.6 6.1 %collective-permute-start.12 = (f32[4,64,128]{2,1,0:T(8,128)S(1)}, f32[4,64,128]{2,1,0:T(8,128)S(1)}, u32[]{:S(2)}, u32[]{:S(2)}) collective-permute-start(f32[4,64,128]{2,1,0:T(8,128)S(1)} %get-tuple-element.56), channel_id=1, source_target_pairs={{8,0},{16,8},{24,16},{32,24},{40,32},{48,40},{56,48},{64,56},{72,6... | collective-permute-start | bytes 393224 | tf_op jit(solution)/shard_map/ppermute | solution.py:21
  109.7 1.9 collective-permute-start.13
  111.6 0.6 dynamic-slice.25
  114.3 0.7 fusion.362
  115.0 6.0 %collective-permute-start.6 = (f32[4,64,128]{2,1,0:T(8,128)}, f32[4,64,128]{2,1,0:T(8,128)S(1)}, u32[]{:S(2)}, u32[]{:S(2)}) collective-permute-start(f32[4,64,128]{2,1,0:T(8,128)} %get-tuple-element.64), channel_id=1, source_target_pairs={{8,0},{16,8},{24,16},{32,24},{40,32},{48,40},{56,48},{64,56},{72,6... | collective-permute-start | bytes 393224 | tf_op jit(solution)/shard_map/ppermute | solution.py:21
  121.1 1.9 collective-permute-start.7
  123.0 2.0 fusion.34
  125.0 15.2 %scatter_fusion.2 = f32[16,64,128]{2,1,0:T(8,128)S(1)} fusion(f32[16,64,128]{2,1,0:T(8,128)S(1)} %fusion.34, s32[256]{0:T(256)S(1)} %bitcast.182, f32[256]{0:T(256)S(1)} %get-tuple-element.126), kind=kCustom, calls=%fused_computation.2 | custom fusion | flops 256 | bytes 6144 | tf_op jit(solution)/shard_map/scatter-add | solution.py:59
  140.2 10.6 %multiply_add_fusion = (f32[16,64,128]{2,1,0:T(8,128)S(1)}, f32[16,64,128]{2,1,0:T(8,128)}, f32[16,64,128]{2,1,0:T(8,128)S(1)}) fusion(f32[16,64,128]{2,1,0:T(8,128)S(1)} %copy-done, f32[16,64,128]{2,1,0:T(8,128)S(1)} %scatter-add.44, f32[16,64,128]{2,1,0:T(8,128)} %copy-done.3, f32[4,64,128]{2,1,0:T(8,128)} %collective-permute-done.7, ...), kind=kLoop, calls=%fused_computation.602 | loop fusion | flops 6553600 | bytes 3932160 | tf_op jit(solution)/shard_map/add | solution.py:86
  150.9 6.1 %collective-permute-start.14 = (f32[4,64,128]{2,1,0:T(8,128)S(1)}, f32[4,64,128]{2,1,0:T(8,128)S(1)}, u32[]{:S(2)}, u32[]{:S(2)}) collective-permute-start(f32[4,64,128]{2,1,0:T(8,128)S(1)} %get-tuple-element.53), channel_id=1, source_target_pairs={{8,0},{16,8},{24,16},{32,24},{40,32},{48,40},{56,48},{64,56},{72,6... | collective-permute-start | bytes 393224 | tf_op jit(solution)/shard_map/ppermute | solution.py:21
  156.9 2.1 collective-permute-start.15
  161.7 0.7 fusion.361
  162.4 6.0 %collective-permute-start.8 = (f32[4,64,128]{2,1,0:T(8,128)}, f32[4,64,128]{2,1,0:T(8,128)S(1)}, u32[]{:S(2)}, u32[]{:S(2)}) collective-permute-start(f32[4,64,128]{2,1,0:T(8,128)} %get-tuple-element.62), channel_id=1, source_target_pairs={{8,0},{16,8},{24,16},{32,24},{40,32},{48,40},{56,48},{64,56},{72,6... | collective-permute-start | bytes 393224 | tf_op jit(solution)/shard_map/ppermute | solution.py:21
  168.5 1.9 collective-permute-start.9
  170.4 2.2 fusion.9
  172.7 15.2 %scatter_fusion.3 = f32[16,64,128]{2,1,0:T(8,128)S(1)} fusion(f32[16,64,128]{2,1,0:T(8,128)S(1)} %fusion.9, s32[256]{0:T(256)S(1)} %bitcast.183, f32[256]{0:T(256)S(1)} %get-tuple-element.43), kind=kCustom, calls=%fused_computation.3 | custom fusion | flops 256 | bytes 6144 | tf_op jit(solution)/shard_map/scatter-add | solution.py:59
  187.9 3.9 fusion.87
  191.9 1.1 fusion.357
  193.0 1.2 convolution_bitcast_fusion
  194.2 1.4 convolution_bitcast_fusion.1
  195.6 48.2 %reduce-scatter.2.cloned.1.call-done = f32[16,8,128]{2,1,0:T(8,128)} async-done(((f32[16,64,128]{2,1,0:T(8,128)}), f32[16,8,128]{2,1,0:T(8,128)}) %reduce-scatter.2.cloned.1.call-update) | async-done | bytes 65552 | tf_op jit(solution)/shard_map/reduce_scatter | solution.py:98
  243.7 0.8 broadcast_multiply_fusion
  245.4 73.3 %psum.7 = f32[12,5]{0,1:T(8,128)S(1)} all-reduce(f32[12,5]{0,1:T(8,128)S(1)} %pad_maximum_fusion.16), channel_id=1, replica_groups=mesh['depth'=32,'shot'=8] {'depth','shot'}, use_global_device_ids=true, to_apply=%region_8.9 | all-reduce | flops 60 | bytes 480 | tf_op jit(solution)/shard_map/psum | solution.py:110
  318.8 0.7 fusion.366
  319.5 0.7 fusion.367
  320.2 0.7 fusion.365
  359.7 0.7 multiply_add_fusion.2
  360.4 29.8 %all_gather.3 = f32[16,64,128]{2,1,0:T(8,128)S(1)} all-gather(f32[16,8,128]{2,1,0:T(8,128)S(1)} %get-tuple-element.41), channel_id=1, replica_groups=mesh['depth'=32,'shot'=8] {'shot'}, dimensions={1}, use_global_device_ids=true | all-gather | bytes 589824 | tf_op jit(solution)/shard_map/all_gather | solution.py:144
  390.3 0.8 copy.49
  (70 shorter events, 2.7 us)
Async XLA Ops:
  7.2 236.6 %reduce-scatter.2.cloned.1.call-start = ((), (), s32[]{:S(2)}) async-start(), calls=%async_computation.1 | async-start | bytes 589824 | tf_op jit(solution)/shard_map/reduce_scatter | solution.py:98
  7.2 20.2 %copy-start.10 = (f32[1,16,64,128]{3,2,1,0:T(8,128)S(1)}, f32[1,16,64,128]{3,2,1,0:T(8,128)}, u32[]{:S(2)}) copy-start(f32[1,16,64,128]{3,2,1,0:T(8,128)} %param.19) | copy-start | bytes 1572868
  8.5 6.1 %copy-start.1 = (f32[1,16,64,128]{3,2,1,0:T(8,128)S(1)}, f32[1,16,64,128]{3,2,1,0:T(8,128)}, u32[]{:S(2)}) copy-start(f32[1,16,64,128]{3,2,1,0:T(8,128)} %param.18) | copy-start | bytes 1572868
  8.6 14.1 %copy-start.14 = (f32[1,4,256]{2,1,0:T(4,128)S(1)}, f32[1,4,256]{2,1,0:T(4,128)}, u32[]{:S(2)}) copy-start(f32[1,4,256]{2,1,0:T(4,128)} %param.24) | copy-start | bytes 12292
  8.6 14.1 %copy-start.15 = (s32[1,256]{1,0:T(1,128)S(1)}, s32[1,256]{1,0:T(1,128)}, u32[]{:S(2)}) copy-start(s32[1,256]{1,0:T(1,128)} %param.23) | copy-start | bytes 3076
  8.6 14.7 %copy-start.13 = (f32[1,4]{1,0:T(1,128)S(1)}, f32[1,4]{1,0:T(1,128)}, u32[]{:S(2)}) copy-start(f32[1,4]{1,0:T(1,128)} %param.22) | copy-start | bytes 52
  8.6 18.1 %copy-start.16 = (s32[3]{0:T(128)S(1)}, s32[3]{0:T(128)}, u32[]{:S(2)}) copy-start(s32[3]{0:T(128)} %constant.255.clone.1) | copy-start | bytes 40
  8.6 18.8 %copy-start.2 = (f32[1,16,64,128]{3,2,1,0:T(8,128)S(1)}, f32[1,16,64,128]{3,2,1,0:T(8,128)}, u32[]{:S(2)}) copy-start(f32[1,16,64,128]{3,2,1,0:T(8,128)} %param.20) | copy-start | bytes 1572868
  8.6 18.8 %collective-permute-start = (f32[4,64,128]{2,1,0:T(8,128)S(1)}, f32[4,64,128]{2,1,0:T(8,128)S(1)}, u32[]{:S(2)}, u32[]{:S(2)}) collective-permute-start(f32[4,64,128]{2,1,0:T(8,128)S(1)} %get-tuple-element.70), channel_id=1, source_target_pairs={{8,0},{16,8},{24,16},{32,24},{40,32},{48,40},{56,48},{64,56},{72,6... | collective-permute-start | bytes 393224 | tf_op jit(solution)/shard_map/ppermute | solution.py:21
  12.7 14.7 %collective-permute-start.1 = (f32[4,64,128]{2,1,0:T(8,128)S(1)}, f32[4,64,128]{2,1,0:T(8,128)S(1)}, u32[]{:S(2)}, u32[]{:S(2)}) collective-permute-start(f32[4,64,128]{2,1,0:T(8,128)S(1)} %get-tuple-element.71), channel_id=1, source_target_pairs={{0,8},{8,16},{16,24},{24,32},{32,40},{40,48},{48,56},{56,64},{64,7... | collective-permute-start | bytes 393224 | tf_op jit(solution)/shard_map/ppermute | solution.py:19
  14.7 38.7 %collective-permute-start.2 = (f32[4,64,128]{2,1,0:T(8,128)S(1)}, f32[4,64,128]{2,1,0:T(8,128)S(1)}, u32[]{:S(2)}, u32[]{:S(2)}) collective-permute-start(f32[4,64,128]{2,1,0:T(8,128)S(1)} %get-tuple-element.68), channel_id=1, source_target_pairs={{8,0},{16,8},{24,16},{32,24},{40,32},{48,40},{56,48},{64,56},{72,6... | collective-permute-start | bytes 393224 | tf_op jit(solution)/shard_map/ppermute | solution.py:21
  20.7 32.6 %collective-permute-start.3 = (f32[4,64,128]{2,1,0:T(8,128)S(1)}, f32[4,64,128]{2,1,0:T(8,128)S(1)}, u32[]{:S(2)}, u32[]{:S(2)}) collective-permute-start(f32[4,64,128]{2,1,0:T(8,128)S(1)} %get-tuple-element.69), channel_id=1, source_target_pairs={{0,8},{8,16},{16,24},{24,32},{32,40},{40,48},{48,56},{56,64},{64,7... | collective-permute-start | bytes 393224 | tf_op jit(solution)/shard_map/ppermute | solution.py:19
  29.4 24.0 %copy-start = (f32[16,64,128]{2,1,0:T(8,128)S(1)}, f32[16,64,128]{2,1,0:T(8,128)}, u32[]{:S(2)}) copy-start(f32[16,64,128]{2,1,0:T(8,128)} %param.16) | copy-start | bytes 1572868
  57.0 19.4 %copy-start.6 = (f32[16,64,128]{2,1,0:T(8,128)}, f32[16,64,128]{2,1,0:T(8,128)S(1)}, u32[]{:S(2)}) copy-start(f32[16,64,128]{2,1,0:T(8,128)S(1)} %get-tuple-element.61) | copy-start | bytes 1572868
  59.8 16.6 %collective-permute-start.10 = (f32[4,64,128]{2,1,0:T(8,128)S(1)}, f32[4,64,128]{2,1,0:T(8,128)S(1)}, u32[]{:S(2)}, u32[]{:S(2)}) collective-permute-start(f32[4,64,128]{2,1,0:T(8,128)S(1)} %get-tuple-element.59), channel_id=1, source_target_pairs={{8,0},{16,8},{24,16},{32,24},{40,32},{48,40},{56,48},{64,56},{72,6... | collective-permute-start | bytes 393224 | tf_op jit(solution)/shard_map/ppermute | solution.py:21
  65.9 10.6 %collective-permute-start.11 = (f32[4,64,128]{2,1,0:T(8,128)S(1)}, f32[4,64,128]{2,1,0:T(8,128)S(1)}, u32[]{:S(2)}, u32[]{:S(2)}) collective-permute-start(f32[4,64,128]{2,1,0:T(8,128)S(1)} %get-tuple-element.60), channel_id=1, source_target_pairs={{0,8},{8,16},{16,24},{24,32},{32,40},{40,48},{48,56},{56,64},{64,7... | collective-permute-start | bytes 393224 | tf_op jit(solution)/shard_map/ppermute | solution.py:19
  68.5 32.4 %collective-permute-start.4 = (f32[4,64,128]{2,1,0:T(8,128)}, f32[4,64,128]{2,1,0:T(8,128)S(1)}, u32[]{:S(2)}, u32[]{:S(2)}) collective-permute-start(f32[4,64,128]{2,1,0:T(8,128)} %get-tuple-element.66), channel_id=1, source_target_pairs={{8,0},{16,8},{24,16},{32,24},{40,32},{48,40},{56,48},{64,56},{72,6... | collective-permute-start | bytes 393224 | tf_op jit(solution)/shard_map/ppermute | solution.py:21
  74.5 26.3 %collective-permute-start.5 = (f32[4,64,128]{2,1,0:T(8,128)S(1)}, f32[4,64,128]{2,1,0:T(8,128)S(1)}, u32[]{:S(2)}, u32[]{:S(2)}) collective-permute-start(f32[4,64,128]{2,1,0:T(8,128)S(1)} %get-tuple-element.67), channel_id=1, source_target_pairs={{0,8},{8,16},{16,24},{24,32},{32,40},{40,48},{48,56},{56,64},{64,7... | collective-permute-start | bytes 393224 | tf_op jit(solution)/shard_map/ppermute | solution.py:19
  103.6 9.3 %copy-start.7 = (f32[16,64,128]{2,1,0:T(8,128)}, f32[16,64,128]{2,1,0:T(8,128)S(1)}, u32[]{:S(2)}) copy-start(f32[16,64,128]{2,1,0:T(8,128)S(1)} %get-tuple-element.58) | copy-start | bytes 1572868
  103.6 19.4 %collective-permute-start.12 = (f32[4,64,128]{2,1,0:T(8,128)S(1)}, f32[4,64,128]{2,1,0:T(8,128)S(1)}, u32[]{:S(2)}, u32[]{:S(2)}) collective-permute-start(f32[4,64,128]{2,1,0:T(8,128)S(1)} %get-tuple-element.56), channel_id=1, source_target_pairs={{8,0},{16,8},{24,16},{32,24},{40,32},{48,40},{56,48},{64,56},{72,6... | collective-permute-start | bytes 393224 | tf_op jit(solution)/shard_map/ppermute | solution.py:21
  109.7 13.3 %collective-permute-start.13 = (f32[4,64,128]{2,1,0:T(8,128)S(1)}, f32[4,64,128]{2,1,0:T(8,128)S(1)}, u32[]{:S(2)}, u32[]{:S(2)}) collective-permute-start(f32[4,64,128]{2,1,0:T(8,128)S(1)} %get-tuple-element.57), channel_id=1, source_target_pairs={{0,8},{8,16},{16,24},{24,32},{32,40},{40,48},{48,56},{56,64},{64,7... | collective-permute-start | bytes 393224 | tf_op jit(solution)/shard_map/ppermute | solution.py:19
  114.3 10.7 %copy-start.3 = (f32[16,64,128]{2,1,0:T(8,128)}, f32[16,64,128]{2,1,0:T(8,128)S(1)}, u32[]{:S(2)}) copy-start(f32[16,64,128]{2,1,0:T(8,128)S(1)} %scatter-add.45) | copy-start | bytes 1572868
  114.3 8.7 %copy-start.8 = (f32[16,64,128]{2,1,0:T(8,128)S(1)}, f32[16,64,128]{2,1,0:T(8,128)}, u32[]{:S(2)}) copy-start(f32[16,64,128]{2,1,0:T(8,128)} %copy-done.7) | copy-start | bytes 1572868
  115.0 25.2 %collective-permute-start.6 = (f32[4,64,128]{2,1,0:T(8,128)}, f32[4,64,128]{2,1,0:T(8,128)S(1)}, u32[]{:S(2)}, u32[]{:S(2)}) collective-permute-start(f32[4,64,128]{2,1,0:T(8,128)} %get-tuple-element.64), channel_id=1, source_target_pairs={{8,0},{16,8},{24,16},{32,24},{40,32},{48,40},{56,48},{64,56},{72,6... | collective-permute-start | bytes 393224 | tf_op jit(solution)/shard_map/ppermute | solution.py:21
  121.1 19.2 %collective-permute-start.7 = (f32[4,64,128]{2,1,0:T(8,128)}, f32[4,64,128]{2,1,0:T(8,128)}, u32[]{:S(2)}, u32[]{:S(2)}) collective-permute-start(f32[4,64,128]{2,1,0:T(8,128)} %get-tuple-element.65), channel_id=1, source_target_pairs={{0,8},{8,16},{16,24},{24,32},{32,40},{40,48},{48,56},{56,64},{64,7... | collective-permute-start | bytes 393224 | tf_op jit(solution)/shard_map/ppermute | solution.py:19
  150.8 9.5 %copy-start.4 = (f32[16,64,128]{2,1,0:T(8,128)}, f32[16,64,128]{2,1,0:T(8,128)S(1)}, u32[]{:S(2)}) copy-start(f32[16,64,128]{2,1,0:T(8,128)S(1)} %get-tuple-element.55) | copy-start | bytes 1572868
  150.9 19.6 %collective-permute-start.14 = (f32[4,64,128]{2,1,0:T(8,128)S(1)}, f32[4,64,128]{2,1,0:T(8,128)S(1)}, u32[]{:S(2)}, u32[]{:S(2)}) collective-permute-start(f32[4,64,128]{2,1,0:T(8,128)S(1)} %get-tuple-element.53), channel_id=1, source_target_pairs={{8,0},{16,8},{24,16},{32,24},{40,32},{48,40},{56,48},{64,56},{72,6... | collective-permute-start | bytes 393224 | tf_op jit(solution)/shard_map/ppermute | solution.py:21
  156.9 13.5 %collective-permute-start.15 = (f32[4,64,128]{2,1,0:T(8,128)S(1)}, f32[4,64,128]{2,1,0:T(8,128)}, u32[]{:S(2)}, u32[]{:S(2)}) collective-permute-start(f32[4,64,128]{2,1,0:T(8,128)S(1)} %get-tuple-element.54), channel_id=1, source_target_pairs={{0,8},{8,16},{16,24},{24,32},{32,40},{40,48},{48,56},{56,64},{64,7... | collective-permute-start | bytes 393224 | tf_op jit(solution)/shard_map/ppermute | solution.py:19
  161.7 8.7 %copy-start.5 = (f32[16,64,128]{2,1,0:T(8,128)S(1)}, f32[16,64,128]{2,1,0:T(8,128)}, u32[]{:S(2)}) copy-start(f32[16,64,128]{2,1,0:T(8,128)} %copy-done.4) | copy-start | bytes 1572868
  162.4 25.5 %collective-permute-start.8 = (f32[4,64,128]{2,1,0:T(8,128)}, f32[4,64,128]{2,1,0:T(8,128)S(1)}, u32[]{:S(2)}, u32[]{:S(2)}) collective-permute-start(f32[4,64,128]{2,1,0:T(8,128)} %get-tuple-element.62), channel_id=1, source_target_pairs={{8,0},{16,8},{24,16},{32,24},{40,32},{48,40},{56,48},{64,56},{72,6... | collective-permute-start | bytes 393224 | tf_op jit(solution)/shard_map/ppermute | solution.py:21
  168.5 19.4 %collective-permute-start.9 = (f32[4,64,128]{2,1,0:T(8,128)}, f32[4,64,128]{2,1,0:T(8,128)S(1)}, u32[]{:S(2)}, u32[]{:S(2)}) collective-permute-start(f32[4,64,128]{2,1,0:T(8,128)} %get-tuple-element.63), channel_id=1, source_target_pairs={{0,8},{8,16},{16,24},{24,32},{32,40},{40,48},{48,56},{56,64},{64,7... | collective-permute-start | bytes 393224 | tf_op jit(solution)/shard_map/ppermute | solution.py:19
  244.6 111.4 %copy-start.12 = (f32[16,8,128]{2,1,0:T(8,128)}, f32[16,8,128]{2,1,0:T(8,128)S(1)}, u32[]{:S(2)}) copy-start(f32[16,8,128]{2,1,0:T(8,128)S(1)} %broadcast_multiply_fusion) | copy-start | bytes 196612
  244.6 115.1 %copy-start.9 = (f32[2,5,16,8,128]{4,3,2,1,0:T(8,128)S(1)}, f32[2,5,16,8,128]{4,3,2,1,0:T(8,128)}, u32[]{:S(2)}) copy-start(f32[2,5,16,8,128]{4,3,2,1,0:T(8,128)} %param.25) | copy-start | bytes 1966084
  244.6 115.1 %copy-start.11 = (f32[16,8,128]{2,1,0:T(8,128)S(1)}, f32[16,8,128]{2,1,0:T(8,128)}, u32[]{:S(2)}) copy-start(f32[16,8,128]{2,1,0:T(8,128)} %reduce-scatter.2.cloned.1.call-done) | copy-start | bytes 196612
Sparse Core Ops, SparseCore 0:
  192.0 51.6 reduce-scatter.1
where the time goes:
time: 400 us; the launch traced here: 398 us
  other arithmetic  111 us (28%)
  blocking collectives  103 us (26%)
  starting transfers between devices  61.9 us (15%)
  between operations  61.9 us (15%)
  waiting for transfers between devices  48.2 us (12%)
  local copies, waits for them, and re-layouts  9.48 us (2%)
    psum x1, blocking collectives, per_device(): packed = lax.psum(packed, ('depth', 'shot'))  73.3 us
    scatter-add x4, other arithmetic, inject(): volume.at[row_safe, remainder // volume.shape[2], remainder % volume.shap...  69.6 us
    reduce_scatter x1, waiting for transfers between devices, per_device(): lax.psum_scatter(summed, 'shot', scatter_dimension=1, tiled=True)  48.2 us
    ppermute x8, starting transfers between devices, with_halo(): lax.ppermute(head, axis, [((i + 1) % count, i) for i in range(ends)])  46.4 us
    all_gather x1, blocking collectives, per_device(): courant_next = lax.all_gather(next_piece, 'shot', axis=1, tiled=True)  29.8 us
    add x3, other arithmetic, per_device(): wave_new = 2.0 * wave_now - wave_old + courant * laplacian  17 us
    ppermute x8, starting transfers between devices, with_halo(): lax.ppermute(tail, axis, [(i, (i + 1) % count) for i in range(ends)])  15.5 us
    add x4, other arithmetic, per_device(): adjoint_new = 2.0 * adjoint_now - adjoint_old + laplace_core(extended)  15.3 us
  transfers between devices with their start and end apart: 17, of which 1 were waited for; matrix products, arithmetic and copies ran while one was open for 24% of the time, Pallas kernels for 0%

commit v1 on v0

--- a/solution.py
+++ b/solution.py
@@ -6,6 +6,12 @@
 STEPS = 4
 PAIRS = 5
 coefficients = (-205.0 / 72.0, 8.0 / 5.0, -1.0 / 5.0, 8.0 / 315.0, -1.0 / 560.0)
+
+
+def get_rates(in_array, net_axis, axis_key):
+    for at in (net_axis, axis_key):
+        in_array = lax.psum(in_array, at)
+    return in_array
 
 
 def with_halo(cells, sides, width):
@@ -107,7 +113,7 @@
     packed = jnp.concatenate(
         [step_change, change_change, step_grad[None], change_grad[None]], axis=0
     )
-    packed = lax.psum(packed, ("depth", "shot"))
+    packed = get_rates(packed, "shot", "depth")
     step_change = packed[:PAIRS]
     change_change = packed[PAIRS : 2 * PAIRS]
     step_grad = packed[2 * PAIRS]

time: 400 us -> 406 us (1.015)
  the two profiles are of different devices: /device:TPU:32 before, /device:TPU:0 now
where the time goes in v1:
time: 406 us; the launch traced here: 405 us
  blocking collectives  112 us (28%)
  other arithmetic  110 us (27%)
  between operations  61.9 us (15%)
  waiting for transfers between devices  55.9 us (14%)
  starting transfers between devices  52.9 us (13%)
  local copies, waits for them, and re-layouts  9.43 us (2%)
    psum x2, blocking collectives, get_rates(): in_array = lax.psum(in_array, at)  81.8 us
    scatter-add x4, other arithmetic, inject(): volume.at[row_safe, remainder // volume.shape[2], remainder % volume.shap...  69.7 us
    reduce_scatter x1, waiting for transfers between devices, per_device(): lax.psum_scatter(summed, 'shot', scatter_dimension=1, tiled=True)  55.8 us
    ppermute x8, starting transfers between devices, with_halo(): lax.ppermute(tail, axis, [(i, (i + 1) % count) for i in range(ends)])  42.4 us
    all_gather x1, blocking collectives, per_device(): courant_next = lax.all_gather(next_piece, 'shot', axis=1, tiled=True)  29.9 us
    add x3, other arithmetic, per_device(): wave_new = 2.0 * wave_now - wave_old + courant * laplacian  16.5 us
    add x4, other arithmetic, per_device(): adjoint_new = 2.0 * adjoint_now - adjoint_old + laplace_core(extended)  15.2 us
    ppermute x8, starting transfers between devices, with_halo(): lax.ppermute(head, axis, [((i + 1) % count, i) for i in range(ends)])  10.4 us
  transfers between devices with their start and end apart: 17, of which 1 were waited for; matrix products, arithmetic and copies ran while one was open for 23% of the time, Pallas kernels for 0%

profile of v1, /device:TPU:0, one launch (start us, length us, event | category | flops | bytes accessed | tf_op | source)
XLA Modules:
  0.0 404.5 jit_solution(11233957375234092933)
XLA Ops:
  7.2 1.3 bitcast_multiply_fusion
  8.6 1.4 collective-permute-start
  10.1 3.0 collective-permute-start.1
  13.2 1.3 collective-permute-start.2
  14.5 3.4 collective-permute-start.3
  21.8 0.7 and_reduce_fusion
  22.5 1.9 fusion.184
  24.5 24.0 %scatter_fusion = f32[16,64,128]{2,1,0:T(8,128)S(1)} fusion(f32[16,64,128]{2,1,0:T(8,128)S(1)} %fusion.184, s32[256]{0:T(256)S(1)} %bitcast.180, f32[256]{0:T(256)} %get-tuple-element.128), kind=kCustom, calls=%fused_computation | custom fusion | flops 256 | bytes 6144 | tf_op jit(solution)/shard_map/scatter-add | solution.py:65
  48.5 3.7 fusion.348
  52.2 0.7 dynamic-slice.24
  54.9 1.3 collective-permute-start.10
  56.2 5.8 %collective-permute-start.11 = (f32[4,64,128]{2,1,0:T(8,128)S(1)}, f32[4,64,128]{2,1,0:T(8,128)S(1)}, u32[]{:S(2)}, u32[]{:S(2)}) collective-permute-start(f32[4,64,128]{2,1,0:T(8,128)S(1)} %get-tuple-element.60), channel_id=1, source_target_pairs={{0,8},{8,16},{16,24},{24,32},{32,40},{40,48},{48,56},{56,64},{64,7... | collective-permute-start | bytes 393224 | tf_op jit(solution)/shard_map/ppermute | solution.py:25
  62.0 0.7 fusion.363
  62.7 1.3 collective-permute-start.4
  64.0 5.8 %collective-permute-start.5 = (f32[4,64,128]{2,1,0:T(8,128)S(1)}, f32[4,64,128]{2,1,0:T(8,128)S(1)}, u32[]{:S(2)}, u32[]{:S(2)}) collective-permute-start(f32[4,64,128]{2,1,0:T(8,128)S(1)} %get-tuple-element.67), channel_id=1, source_target_pairs={{0,8},{8,16},{16,24},{24,32},{32,40},{40,48},{48,56},{56,64},{64,7... | collective-permute-start | bytes 393224 | tf_op jit(solution)/shard_map/ppermute | solution.py:25
  69.8 9.1 %fusion.59 = f32[16,64,128]{2,1,0:T(8,128)S(1)} fusion(f32[16,64,128]{2,1,0:T(8,128)} %copy-done.6, f32[4,64,128]{2,1,0:T(8,128)S(1)} %collective-permute-done.11, f32[4,64,128]{2,1,0:T(8,128)S(1)} %collective-permute-done.10, f32[1,16,64,128]{3,2,1,0:T(8,128)S(1)} %copy-done.2, f32[16,64,128]{2,1,0:T(8,128)S(1)} %scatter_fusion), kind=kLoop, calls=%fused_computation.289 | loop fusion | flops 6291456 | bytes 2359296 | tf_op jit(solution)/shard_map/add | solution.py:100
  78.9 15.2 %scatter_fusion.1 = f32[16,64,128]{2,1,0:T(8,128)S(1)} fusion(f32[16,64,128]{2,1,0:T(8,128)S(1)} %fusion.59, s32[256]{0:T(256)S(1)} %bitcast.181, f32[256]{0:T(256)S(1)} %get-tuple-element.127), kind=kCustom, calls=%fused_computation.1 | custom fusion | flops 256 | bytes 6144 | tf_op jit(solution)/shard_map/scatter-add | solution.py:65
  94.2 2.7 multiply_add_fusion.1
  96.9 1.3 collective-permute-start.12
  98.2 5.8 %collective-permute-start.13 = (f32[4,64,128]{2,1,0:T(8,128)S(1)}, f32[4,64,128]{2,1,0:T(8,128)S(1)}, u32[]{:S(2)}, u32[]{:S(2)}) collective-permute-start(f32[4,64,128]{2,1,0:T(8,128)S(1)} %get-tuple-element.57), channel_id=1, source_target_pairs={{0,8},{8,16},{16,24},{24,32},{32,40},{40,48},{48,56},{56,64},{64,7... | collective-permute-start | bytes 393224 | tf_op jit(solution)/shard_map/ppermute | solution.py:25
  104.0 0.6 dynamic-slice.25
  106.7 0.7 fusion.362
  107.4 1.3 collective-permute-start.6
  108.7 6.4 %collective-permute-start.7 = (f32[4,64,128]{2,1,0:T(8,128)}, f32[4,64,128]{2,1,0:T(8,128)}, u32[]{:S(2)}, u32[]{:S(2)}) collective-permute-start(f32[4,64,128]{2,1,0:T(8,128)} %get-tuple-element.65), channel_id=1, source_target_pairs={{0,8},{8,16},{16,24},{24,32},{32,40},{40,48},{48,56},{56,64},{64,7... | collective-permute-start | bytes 393224 | tf_op jit(solution)/shard_map/ppermute | solution.py:25
  115.1 2.0 fusion.34
  117.1 15.2 %scatter_fusion.2 = f32[16,64,128]{2,1,0:T(8,128)S(1)} fusion(f32[16,64,128]{2,1,0:T(8,128)S(1)} %fusion.34, s32[256]{0:T(256)S(1)} %bitcast.182, f32[256]{0:T(256)S(1)} %get-tuple-element.126), kind=kCustom, calls=%fused_computation.2 | custom fusion | flops 256 | bytes 6144 | tf_op jit(solution)/shard_map/scatter-add | solution.py:65
  132.4 10.1 %multiply_add_fusion = (f32[16,64,128]{2,1,0:T(8,128)S(1)}, f32[16,64,128]{2,1,0:T(8,128)}, f32[16,64,128]{2,1,0:T(8,128)S(1)}) fusion(f32[16,64,128]{2,1,0:T(8,128)S(1)} %copy-done, f32[16,64,128]{2,1,0:T(8,128)S(1)} %scatter-add.44, f32[16,64,128]{2,1,0:T(8,128)} %copy-done.3, f32[4,64,128]{2,1,0:T(8,128)} %collective-permute-done.7, ...), kind=kLoop, calls=%fused_computation.602 | loop fusion | flops 6553600 | bytes 3932160 | tf_op jit(solution)/shard_map/add | solution.py:92
  142.6 1.3 collective-permute-start.14
  143.9 6.0 %collective-permute-start.15 = (f32[4,64,128]{2,1,0:T(8,128)S(1)}, f32[4,64,128]{2,1,0:T(8,128)}, u32[]{:S(2)}, u32[]{:S(2)}) collective-permute-start(f32[4,64,128]{2,1,0:T(8,128)S(1)} %get-tuple-element.54), channel_id=1, source_target_pairs={{0,8},{8,16},{16,24},{24,32},{32,40},{40,48},{48,56},{56,64},{64,7... | collective-permute-start | bytes 393224 | tf_op jit(solution)/shard_map/ppermute | solution.py:25
  152.5 0.7 fusion.361
  153.2 1.3 collective-permute-start.8
  154.5 6.2 %collective-permute-start.9 = (f32[4,64,128]{2,1,0:T(8,128)}, f32[4,64,128]{2,1,0:T(8,128)S(1)}, u32[]{:S(2)}, u32[]{:S(2)}) collective-permute-start(f32[4,64,128]{2,1,0:T(8,128)} %get-tuple-element.63), channel_id=1, source_target_pairs={{0,8},{8,16},{16,24},{24,32},{32,40},{40,48},{48,56},{56,64},{64,7... | collective-permute-start | bytes 393224 | tf_op jit(solution)/shard_map/ppermute | solution.py:25
  160.8 2.2 fusion.9
  163.0 15.2 %scatter_fusion.3 = f32[16,64,128]{2,1,0:T(8,128)S(1)} fusion(f32[16,64,128]{2,1,0:T(8,128)S(1)} %fusion.9, s32[256]{0:T(256)S(1)} %bitcast.183, f32[256]{0:T(256)S(1)} %get-tuple-element.43), kind=kCustom, calls=%fused_computation.3 | custom fusion | flops 256 | bytes 6144 | tf_op jit(solution)/shard_map/scatter-add | solution.py:65
  178.3 3.9 fusion.87
  182.2 1.1 fusion.357
  183.4 1.2 convolution_bitcast_fusion
  184.6 1.4 convolution_bitcast_fusion.1
  185.9 55.8 %reduce-scatter.2.cloned.1.call-done = f32[16,8,128]{2,1,0:T(8,128)} async-done(((f32[16,64,128]{2,1,0:T(8,128)}), f32[16,8,128]{2,1,0:T(8,128)}) %reduce-scatter.2.cloned.1.call-update) | async-done | bytes 65552 | tf_op jit(solution)/shard_map/reduce_scatter | solution.py:104
  241.8 0.8 broadcast_multiply_fusion
  243.4 16.8 %psum.14 = f32[12,5]{0,1:T(8,128)S(1)} all-reduce(f32[12,5]{0,1:T(8,128)S(1)} %pad_maximum_fusion.16), channel_id=1, replica_groups=mesh['depth'=32,'shot'=8] {'shot'}, use_global_device_ids=true, to_apply=%region_8.9 | all-reduce | flops 60 | bytes 480 | tf_op jit(solution)/shard_map/psum | solution.py:13
  260.2 65.0 %psum.15 = f32[12,5]{0,1:T(8,128)S(1)} all-reduce(f32[12,5]{0,1:T(8,128)S(1)} %psum.14), channel_id=1, replica_groups=mesh['depth'=32,'shot'=8] {'depth'}, use_global_device_ids=true, to_apply=%region_9.10 | all-reduce | flops 60 | bytes 480 | tf_op jit(solution)/shard_map/psum | solution.py:13
  325.3 0.7 fusion.366
  326.0 0.7 fusion.367
  326.7 0.7 fusion.365
  366.3 0.7 multiply_add_fusion.2
  367.0 29.9 %all_gather.3 = f32[16,64,128]{2,1,0:T(8,128)S(1)} all-gather(f32[16,8,128]{2,1,0:T(8,128)S(1)} %get-tuple-element.41), channel_id=1, replica_groups=mesh['depth'=32,'shot'=8] {'shot'}, dimensions={1}, use_global_device_ids=true | all-gather | bytes 589824 | tf_op jit(solution)/shard_map/all_gather | solution.py:150
  396.9 0.8 copy.49
  (71 shorter events, 3.3 us)
Async XLA Ops:
  7.2 234.6 %reduce-scatter.2.cloned.1.call-start = ((), (), s32[]{:S(2)}) async-start(), calls=%async_computation.1 | async-start | bytes 589824 | tf_op jit(solution)/shard_map/reduce_scatter | solution.py:104
  7.2 15.3 %copy-start.10 = (f32[1,16,64,128]{3,2,1,0:T(8,128)S(1)}, f32[1,16,64,128]{3,2,1,0:T(8,128)}, u32[]{:S(2)}) copy-start(f32[1,16,64,128]{3,2,1,0:T(8,128)} %param.19) | copy-start | bytes 1572868
  8.5 4.6 %copy-start.1 = (f32[1,16,64,128]{3,2,1,0:T(8,128)S(1)}, f32[1,16,64,128]{3,2,1,0:T(8,128)}, u32[]{:S(2)}) copy-start(f32[1,16,64,128]{3,2,1,0:T(8,128)} %param.18) | copy-start | bytes 1572868
  8.6 9.4 %copy-start.14 = (f32[1,4,256]{2,1,0:T(4,128)S(1)}, f32[1,4,256]{2,1,0:T(4,128)}, u32[]{:S(2)}) copy-start(f32[1,4,256]{2,1,0:T(4,128)} %param.24) | copy-start | bytes 12292
  8.6 9.4 %copy-start.15 = (s32[1,256]{1,0:T(1,128)S(1)}, s32[1,256]{1,0:T(1,128)}, u32[]{:S(2)}) copy-start(s32[1,256]{1,0:T(1,128)} %param.23) | copy-start | bytes 3076
  8.6 10.0 %copy-start.13 = (f32[1,4]{1,0:T(1,128)S(1)}, f32[1,4]{1,0:T(1,128)}, u32[]{:S(2)}) copy-start(f32[1,4]{1,0:T(1,128)} %param.22) | copy-start | bytes 52
  8.6 13.2 %copy-start.16 = (s32[3]{0:T(128)S(1)}, s32[3]{0:T(128)}, u32[]{:S(2)}) copy-start(s32[3]{0:T(128)} %constant.255.clone.1) | copy-start | bytes 40
  8.6 13.9 %copy-start.2 = (f32[1,16,64,128]{3,2,1,0:T(8,128)S(1)}, f32[1,16,64,128]{3,2,1,0:T(8,128)}, u32[]{:S(2)}) copy-start(f32[1,16,64,128]{3,2,1,0:T(8,128)} %param.20) | copy-start | bytes 1572868
  8.6 13.9 %collective-permute-start = (f32[4,64,128]{2,1,0:T(8,128)S(1)}, f32[4,64,128]{2,1,0:T(8,128)S(1)}, u32[]{:S(2)}, u32[]{:S(2)}) collective-permute-start(f32[4,64,128]{2,1,0:T(8,128)S(1)} %get-tuple-element.70), channel_id=1, source_target_pairs={{8,0},{16,8},{24,16},{32,24},{40,32},{48,40},{56,48},{64,56},{72,6... | collective-permute-start | bytes 393224 | tf_op jit(solution)/shard_map/ppermute | solution.py:27
  10.1 12.4 %collective-permute-start.1 = (f32[4,64,128]{2,1,0:T(8,128)S(1)}, f32[4,64,128]{2,1,0:T(8,128)S(1)}, u32[]{:S(2)}, u32[]{:S(2)}) collective-permute-start(f32[4,64,128]{2,1,0:T(8,128)S(1)} %get-tuple-element.71), channel_id=1, source_target_pairs={{0,8},{8,16},{16,24},{24,32},{32,40},{40,48},{48,56},{56,64},{64,7... | collective-permute-start | bytes 393224 | tf_op jit(solution)/shard_map/ppermute | solution.py:25
  13.2 35.3 %collective-permute-start.2 = (f32[4,64,128]{2,1,0:T(8,128)S(1)}, f32[4,64,128]{2,1,0:T(8,128)S(1)}, u32[]{:S(2)}, u32[]{:S(2)}) collective-permute-start(f32[4,64,128]{2,1,0:T(8,128)S(1)} %get-tuple-element.68), channel_id=1, source_target_pairs={{8,0},{16,8},{24,16},{32,24},{40,32},{48,40},{56,48},{64,56},{72,6... | collective-permute-start | bytes 393224 | tf_op jit(solution)/shard_map/ppermute | solution.py:27
  14.5 34.0 %collective-permute-start.3 = (f32[4,64,128]{2,1,0:T(8,128)S(1)}, f32[4,64,128]{2,1,0:T(8,128)S(1)}, u32[]{:S(2)}, u32[]{:S(2)}) collective-permute-start(f32[4,64,128]{2,1,0:T(8,128)S(1)} %get-tuple-element.69), channel_id=1, source_target_pairs={{0,8},{8,16},{16,24},{24,32},{32,40},{40,48},{48,56},{56,64},{64,7... | collective-permute-start | bytes 393224 | tf_op jit(solution)/shard_map/ppermute | solution.py:25
  24.5 24.0 %copy-start = (f32[16,64,128]{2,1,0:T(8,128)S(1)}, f32[16,64,128]{2,1,0:T(8,128)}, u32[]{:S(2)}) copy-start(f32[16,64,128]{2,1,0:T(8,128)} %param.16) | copy-start | bytes 1572868
  52.2 17.6 %copy-start.6 = (f32[16,64,128]{2,1,0:T(8,128)}, f32[16,64,128]{2,1,0:T(8,128)S(1)}, u32[]{:S(2)}) copy-start(f32[16,64,128]{2,1,0:T(8,128)S(1)} %get-tuple-element.61) | copy-start | bytes 1572868
  54.9 14.8 %collective-permute-start.10 = (f32[4,64,128]{2,1,0:T(8,128)S(1)}, f32[4,64,128]{2,1,0:T(8,128)S(1)}, u32[]{:S(2)}, u32[]{:S(2)}) collective-permute-start(f32[4,64,128]{2,1,0:T(8,128)S(1)} %get-tuple-element.59), channel_id=1, source_target_pairs={{8,0},{16,8},{24,16},{32,24},{40,32},{48,40},{56,48},{64,56},{72,6... | collective-permute-start | bytes 393224 | tf_op jit(solution)/shard_map/ppermute | solution.py:27
  56.2 13.5 %collective-permute-start.11 = (f32[4,64,128]{2,1,0:T(8,128)S(1)}, f32[4,64,128]{2,1,0:T(8,128)S(1)}, u32[]{:S(2)}, u32[]{:S(2)}) collective-permute-start(f32[4,64,128]{2,1,0:T(8,128)S(1)} %get-tuple-element.60), channel_id=1, source_target_pairs={{0,8},{8,16},{16,24},{24,32},{32,40},{40,48},{48,56},{56,64},{64,7... | collective-permute-start | bytes 393224 | tf_op jit(solution)/shard_map/ppermute | solution.py:25
  62.7 31.5 %collective-permute-start.4 = (f32[4,64,128]{2,1,0:T(8,128)}, f32[4,64,128]{2,1,0:T(8,128)S(1)}, u32[]{:S(2)}, u32[]{:S(2)}) collective-permute-start(f32[4,64,128]{2,1,0:T(8,128)} %get-tuple-element.66), channel_id=1, source_target_pairs={{8,0},{16,8},{24,16},{32,24},{40,32},{48,40},{56,48},{64,56},{72,6... | collective-permute-start | bytes 393224 | tf_op jit(solution)/shard_map/ppermute | solution.py:27
  64.0 30.2 %collective-permute-start.5 = (f32[4,64,128]{2,1,0:T(8,128)S(1)}, f32[4,64,128]{2,1,0:T(8,128)S(1)}, u32[]{:S(2)}, u32[]{:S(2)}) collective-permute-start(f32[4,64,128]{2,1,0:T(8,128)S(1)} %get-tuple-element.67), channel_id=1, source_target_pairs={{0,8},{8,16},{16,24},{24,32},{32,40},{40,48},{48,56},{56,64},{64,7... | collective-permute-start | bytes 393224 | tf_op jit(solution)/shard_map/ppermute | solution.py:25
  96.9 8.3 %copy-start.7 = (f32[16,64,128]{2,1,0:T(8,128)}, f32[16,64,128]{2,1,0:T(8,128)S(1)}, u32[]{:S(2)}) copy-start(f32[16,64,128]{2,1,0:T(8,128)S(1)} %get-tuple-element.58) | copy-start | bytes 1572868
  96.9 18.2 %collective-permute-start.12 = (f32[4,64,128]{2,1,0:T(8,128)S(1)}, f32[4,64,128]{2,1,0:T(8,128)S(1)}, u32[]{:S(2)}, u32[]{:S(2)}) collective-permute-start(f32[4,64,128]{2,1,0:T(8,128)S(1)} %get-tuple-element.56), channel_id=1, source_target_pairs={{8,0},{16,8},{24,16},{32,24},{40,32},{48,40},{56,48},{64,56},{72,6... | collective-permute-start | bytes 393224 | tf_op jit(solution)/shard_map/ppermute | solution.py:27
  98.2 16.9 %collective-permute-start.13 = (f32[4,64,128]{2,1,0:T(8,128)S(1)}, f32[4,64,128]{2,1,0:T(8,128)S(1)}, u32[]{:S(2)}, u32[]{:S(2)}) collective-permute-start(f32[4,64,128]{2,1,0:T(8,128)S(1)} %get-tuple-element.57), channel_id=1, source_target_pairs={{0,8},{8,16},{16,24},{24,32},{32,40},{40,48},{48,56},{56,64},{64,7... | collective-permute-start | bytes 393224 | tf_op jit(solution)/shard_map/ppermute | solution.py:25
  106.7 10.4 %copy-start.3 = (f32[16,64,128]{2,1,0:T(8,128)}, f32[16,64,128]{2,1,0:T(8,128)S(1)}, u32[]{:S(2)}) copy-start(f32[16,64,128]{2,1,0:T(8,128)S(1)} %scatter-add.45) | copy-start | bytes 1572868
  106.7 8.4 %copy-start.8 = (f32[16,64,128]{2,1,0:T(8,128)S(1)}, f32[16,64,128]{2,1,0:T(8,128)}, u32[]{:S(2)}) copy-start(f32[16,64,128]{2,1,0:T(8,128)} %copy-done.7) | copy-start | bytes 1572868
  107.4 25.0 %collective-permute-start.6 = (f32[4,64,128]{2,1,0:T(8,128)}, f32[4,64,128]{2,1,0:T(8,128)S(1)}, u32[]{:S(2)}, u32[]{:S(2)}) collective-permute-start(f32[4,64,128]{2,1,0:T(8,128)} %get-tuple-element.64), channel_id=1, source_target_pairs={{8,0},{16,8},{24,16},{32,24},{40,32},{48,40},{56,48},{64,56},{72,6... | collective-permute-start | bytes 393224 | tf_op jit(solution)/shard_map/ppermute | solution.py:27
  108.7 23.7 %collective-permute-start.7 = (f32[4,64,128]{2,1,0:T(8,128)}, f32[4,64,128]{2,1,0:T(8,128)}, u32[]{:S(2)}, u32[]{:S(2)}) collective-permute-start(f32[4,64,128]{2,1,0:T(8,128)} %get-tuple-element.65), channel_id=1, source_target_pairs={{0,8},{8,16},{16,24},{24,32},{32,40},{40,48},{48,56},{56,64},{64,7... | collective-permute-start | bytes 393224 | tf_op jit(solution)/shard_map/ppermute | solution.py:25
  142.5 8.5 %copy-start.4 = (f32[16,64,128]{2,1,0:T(8,128)}, f32[16,64,128]{2,1,0:T(8,128)S(1)}, u32[]{:S(2)}) copy-start(f32[16,64,128]{2,1,0:T(8,128)S(1)} %get-tuple-element.55) | copy-start | bytes 1572868
  142.6 18.2 %collective-permute-start.14 = (f32[4,64,128]{2,1,0:T(8,128)S(1)}, f32[4,64,128]{2,1,0:T(8,128)S(1)}, u32[]{:S(2)}, u32[]{:S(2)}) collective-permute-start(f32[4,64,128]{2,1,0:T(8,128)S(1)} %get-tuple-element.53), channel_id=1, source_target_pairs={{8,0},{16,8},{24,16},{32,24},{40,32},{48,40},{56,48},{64,56},{72,6... | collective-permute-start | bytes 393224 | tf_op jit(solution)/shard_map/ppermute | solution.py:27
  143.9 16.9 %collective-permute-start.15 = (f32[4,64,128]{2,1,0:T(8,128)S(1)}, f32[4,64,128]{2,1,0:T(8,128)}, u32[]{:S(2)}, u32[]{:S(2)}) collective-permute-start(f32[4,64,128]{2,1,0:T(8,128)S(1)} %get-tuple-element.54), channel_id=1, source_target_pairs={{0,8},{8,16},{16,24},{24,32},{32,40},{40,48},{48,56},{56,64},{64,7... | collective-permute-start | bytes 393224 | tf_op jit(solution)/shard_map/ppermute | solution.py:25
  152.5 8.3 %copy-start.5 = (f32[16,64,128]{2,1,0:T(8,128)S(1)}, f32[16,64,128]{2,1,0:T(8,128)}, u32[]{:S(2)}) copy-start(f32[16,64,128]{2,1,0:T(8,128)} %copy-done.4) | copy-start | bytes 1572868
  153.2 25.0 %collective-permute-start.8 = (f32[4,64,128]{2,1,0:T(8,128)}, f32[4,64,128]{2,1,0:T(8,128)S(1)}, u32[]{:S(2)}, u32[]{:S(2)}) collective-permute-start(f32[4,64,128]{2,1,0:T(8,128)} %get-tuple-element.62), channel_id=1, source_target_pairs={{8,0},{16,8},{24,16},{32,24},{40,32},{48,40},{56,48},{64,56},{72,6... | collective-permute-start | bytes 393224 | tf_op jit(solution)/shard_map/ppermute | solution.py:27
  154.5 23.8 %collective-permute-start.9 = (f32[4,64,128]{2,1,0:T(8,128)}, f32[4,64,128]{2,1,0:T(8,128)S(1)}, u32[]{:S(2)}, u32[]{:S(2)}) collective-permute-start(f32[4,64,128]{2,1,0:T(8,128)} %get-tuple-element.63), channel_id=1, source_target_pairs={{0,8},{8,16},{16,24},{24,32},{32,40},{40,48},{48,56},{56,64},{64,7... | collective-permute-start | bytes 393224 | tf_op jit(solution)/shard_map/ppermute | solution.py:25
  242.6 119.9 %copy-start.12 = (f32[16,8,128]{2,1,0:T(8,128)}, f32[16,8,128]{2,1,0:T(8,128)S(1)}, u32[]{:S(2)}) copy-start(f32[16,8,128]{2,1,0:T(8,128)S(1)} %broadcast_multiply_fusion) | copy-start | bytes 196612
  242.6 123.6 %copy-start.9 = (f32[2,5,16,8,128]{4,3,2,1,0:T(8,128)S(1)}, f32[2,5,16,8,128]{4,3,2,1,0:T(8,128)}, u32[]{:S(2)}) copy-start(f32[2,5,16,8,128]{4,3,2,1,0:T(8,128)} %param.25) | copy-start | bytes 1966084
  242.7 123.6 %copy-start.11 = (f32[16,8,128]{2,1,0:T(8,128)S(1)}, f32[16,8,128]{2,1,0:T(8,128)}, u32[]{:S(2)}) copy-start(f32[16,8,128]{2,1,0:T(8,128)} %reduce-scatter.2.cloned.1.call-done) | copy-start | bytes 196612
Sparse Core Ops, SparseCore 0:
  182.4 59.3 reduce-scatter.1
